TPU v7x, 32 devices: a whole 2x2x4 slice. The times are simulated.
32 devices in a mesh: sx: 16 (over z, y, x), sy: 2 (over core).
Axes of the slice: x: 2, y: 2, z: 4, core: 2. Of those that a mesh axis runs over, the one named last changes fastest.
Arguments:
- snapshots: bfloat16 [1024, 3, 32, 256], P(None, None, 'sx', 'sy'), may hold values from -6 to 6
- quad_weight: float32 [3, 32, 256], P(None, 'sx', 'sy'), may hold values from 0.5 to 1200
- mode_guess: float32 [16, 64, 2, 8], replicated, may hold values from -6 to 6
- bins: int32 [16], replicated, may hold values from 1 to 127
- starts: int32 [64], replicated, may hold values from 0 to 768
Outputs:
- modes: float32 [16, 2, 8, 3, 32, 256], P(None, None, None, None, 'sx', 'sy')
- energy: float32 [16, 8], replicated
All inputs are finite; a program needn't handle non-finite values.
Results may differ from a plain program's by a relative error of at most 0.0024.
Values may be sent and summed in bfloat16 or wider, within the bound.
A program may use at most 64 MiB of HBM per device.

v0:
```python
import functools
import jax
import jax.numpy as jnp
from jax import lax
from jax.experimental import pallas as pl
from jax.experimental.pallas import tpu as pltpu
from jax.sharding import PartitionSpec as P

NFFT = 256
LANES = 128
EPS = 1e-06
MESH = pl.DeviceIdType.MESH


def fill_twiddle(bins, nbins, tw):
    shape = (nbins, NFFT)
    row = lax.broadcasted_iota(jnp.int32, shape, 0)
    step = lax.broadcasted_iota(jnp.int32, shape, 1)
    number = jnp.zeros(shape, jnp.int32)
    for f in range(nbins):
        number = jnp.where(row == f, bins[f], number)
    turn = 2.0 * jnp.pi / NFFT
    window = 0.5 - 0.5 * jnp.cos(step.astype(jnp.float32) * turn)
    norm_c = lax.rsqrt(jnp.sum(window * window, axis=1, keepdims=True))
    phase = lax.rem(number * step, NFFT)
    angle = phase.astype(jnp.float32) * turn
    tw[:nbins, :] = norm_c * window * jnp.cos(angle)
    tw[nbins:, :] = -(norm_c * window) * jnp.sin(angle)


def shifted_rows(start, nq, length, tw):
    tile = start // LANES
    shift = start - tile * LANES
    wide = lax.broadcasted_iota(jnp.int32, (nq, LANES), 1)
    keep = wide < shift
    zero = jnp.zeros((nq, LANES), jnp.float32)
    prev, pieces = zero, []
    for j in range(NFFT // LANES):
        cur = pltpu.roll(tw[:, j * LANES:(j + 1) * LANES], shift, 1)
        pieces.append(jnp.where(keep, prev, cur))
        prev = cur
    pieces.append(jnp.where(keep, prev, zero))
    outs = []
    for j in range(length // LANES):
        out = zero
        for i, piece in enumerate(pieces):
            out = jnp.where(tile + i == j, piece, out)
        outs.append(out)
    return jnp.concatenate(outs, axis=1).astype(jnp.bfloat16)


def split2(value):
    high = value.astype(jnp.bfloat16)
    low = (value - high.astype(jnp.float32)).astype(jnp.bfloat16)
    return jnp.concatenate([high, low], axis=0)


def main_kernel(dims, starts_hbm, bins_hbm, x_hbm, quad_hbm, guess_hbm, y_ref, z_ref,
                starts, bins, x_ref, quad_ref, guess_ref, t_ref, tw, xs, xr, sq, qs,
                w_ref, acc, sqbuf, zsend, zrecv, zall, load_sems, sems):
    (length, nvar, ctile, nblock, nbins, nmode, n_x, n_y, per, grid_points) = dims
    n = n_x * n_y
    me = lax.axis_index("sx") * n_y + lax.axis_index("sy")
    per_var = ctile // nvar
    nq = 2 * nbins
    loads = [
        pltpu.make_async_copy(src, dst, load_sems.at[i])
        for i, (src, dst) in enumerate(
            [
                (bins_hbm, bins),
                (starts_hbm, starts),
                (quad_hbm, quad_ref),
                (x_hbm, x_ref),
                (guess_hbm, guess_ref),
            ]
        )
    ]
    for load in loads:
        load.start()

    ix, iy = lax.axis_index("sx"), lax.axis_index("sy")

    def each_partner(act):
        def pick(dx, dy):
            tx, ty = lax.rem(ix + dx, n_x), lax.rem(iy + dy, n_y)
            act(tx * n_y + ty, (tx, ty))

        for dy in range(1, n_y):
            pick(0, dy)

        def go(dx, carry):
            for dy in range(n_y):
                pick(dx, dy)
            return carry

        lax.fori_loop(1, n_x, go, 0, unroll=5)

    barrier = pltpu.get_barrier_semaphore()
    each_partner(
        lambda t, where: pl.semaphore_signal(
            barrier, inc=1, device_id=where, device_id_type=MESH
        )
    )

    def spread(src, dst, phase, by_target):
        each_partner(
            lambda t, where: pltpu.make_async_remote_copy(
                src_ref=src.at[t] if by_target else src,
                dst_ref=dst.at[me],
                send_sem=sems.at[2 * phase],
                recv_sem=sems.at[2 * phase + 1],
                device_id=where,
                device_id_type=MESH,
            ).start()
        )

    def wait_all(dst, sem):
        rest = dst.at[pl.ds(0, n - 1)]
        pltpu.make_async_copy(rest, rest, sems.at[sem]).wait()

    loads[0].wait()
    fill_twiddle(bins, nbins, tw)
    for load in loads[1:]:
        load.wait()
    rows = x_ref.shape[0]
    step = rows // 16

    @pl.loop(0, 16)
    def _(i):
        at = pl.ds(pl.multiple_of(i * step, step), step)
        xs[at, :] = x_ref[at, :].astype(jnp.float32)

    lane = lax.broadcasted_iota(jnp.int32, (1, LANES), 1)
    quads = [quad_ref[c // per_var, c % per_var:c % per_var + 1, :] for c in range(ctile)]
    total = jnp.zeros((1, LANES), jnp.float32)
    for c in range(ctile):
        col = xs[pl.ds(c, length, stride=ctile), :]
        xr[:, c * LANES:(c + 1) * LANES] = col.astype(jnp.bfloat16)
        sums = jnp.sum(col * col, axis=0, keepdims=True) * quads[c]
        one = jnp.sum(sums, axis=1, keepdims=True)
        total = total + jnp.where(lane == c // per_var, one, 0.0)
    sq[...] = total

    for f in range(nbins):
        g_re, g_im = guess_ref[f, 0], guess_ref[f, 1]
        w_ref[f] = split2(
            jnp.concatenate(
                [
                    jnp.concatenate([g_re, -g_im], axis=1),
                    jnp.concatenate([g_im, g_re], axis=1),
                ],
                axis=0,
            )
        )

    pl.semaphore_wait(barrier, n - 1)
    spread(sq, sqbuf, 0, False)

    @pl.loop(0, nblock // 4)
    def _(i):
        for k in range(4):
            b = i * 4 + k
            t_ref[pl.ds(pl.multiple_of(b * nq, nq), nq), :] = shifted_rows(
                starts[b], nq, length, tw
            )

    chunks = 4
    chunk = nblock * nq // chunks

    def transform(i, j):
        at = slice(i * chunk, (i + 1) * chunk)
        out = jnp.dot(
            t_ref[at, :],
            xr[:, 2 * j * LANES:2 * (j + 1) * LANES],
            preferred_element_type=jnp.float32,
        )
        qs[2 * j, at, :] = out[:, :LANES]
        qs[2 * j + 1, at, :] = out[:, LANES:]

    def fold(value):
        return value[:2 * nmode] + value[2 * nmode:]

    def project(f, j, cols):
        for c in (2 * j, 2 * j + 1):
            for p in range(2):
                part = qs[c, pl.ds(p * nbins + f, nblock, stride=nq), :]
                y_ref[f, p * nblock:(p + 1) * nblock, c * LANES:(c + 1) * LANES] = (
                    part * cols[c]
                ).astype(jnp.bfloat16)
        y = y_ref[f, :, 2 * j * LANES:2 * (j + 1) * LANES]
        u = fold(jnp.dot(w_ref[f], y, preferred_element_type=jnp.float32))
        return fold(
            lax.dot_general(
                split2(u), y, (((1,), (1,)), ((), ())), preferred_element_type=jnp.float32
            )
        )

    pairs = ctile // 2
    share = nbins // chunks
    for i in range(chunks):
        transform(i, 0)

    wait_all(sqbuf, 1)
    sqbuf[me] = sq[...]
    total = jnp.sum(sqbuf[...], axis=0)
    scale = lax.rsqrt(total / (length * grid_points) + EPS)
    cols = []
    for c in range(ctile):
        one = jnp.sum(jnp.where(lane == c // per_var, scale, 0.0), axis=1, keepdims=True)
        cols.append(one * jnp.sqrt(quads[c]))

    for j in range(1, pairs):
        for i in range(chunks):
            transform(i, j)
            for f in range(i * share, (i + 1) * share):
                a = project(f, j - 1, cols)
                acc[f] = a if j == 1 else acc[f] + a

    low_half = lax.broadcasted_iota(jnp.int32, (nmode, LANES), 1) < nblock
    parts = nmode // per
    for f in range(nbins):
        a = project(f, pairs - 1, cols)
        if pairs > 1:
            a = a + acc[f]
        a = a * (1.0 / (3.0 * grid_points))
        up = a[:nmode]
        z = pltpu.roll(a[nmode:], nblock, 1) + jnp.where(low_half, up, -up)
        for s in range(parts):
            zsend[f * parts + s] = z[s * per:(s + 1) * per]
    owners = nbins * parts
    for s in range(owners, n):
        zsend[s] = jnp.zeros((per, LANES), jnp.float32)

    spread(zsend, zrecv, 1, True)
    wait_all(zrecv, 3)
    zrecv[me] = zsend[me]
    zall[me] = jnp.sum(zrecv[...], axis=0)
    spread(zall.at[me], zall, 2, False)
    wait_all(zall, 5)
    for s in range(owners):
        z_ref[s * per:(s + 1) * per] = zall[s]
    wait_all(zrecv, 2)
    wait_all(zall, 4)
    wait_all(sqbuf, 0)


def modes_kernel(dims, y_ref, z_ref, modes_hbm, energy_ref, out, sems):
    ctile, nblock, nbins, nmode = dims
    span = 2 * nmode * ctile
    low_half = lax.broadcasted_iota(jnp.int32, (nmode, LANES), 1) < nblock
    column = lax.broadcasted_iota(jnp.int32, (nmode, nbins), 1)
    energy = jnp.zeros((nmode, nbins), jnp.float32)

    def store(f):
        at = pl.ds(f * span, span)
        return pltpu.make_async_copy(out.at[at], modes_hbm.at[at], sems.at[f])

    for f in range(nbins):
        z = z_ref[f * nmode:(f + 1) * nmode]
        norms = jnp.sum(z * z, axis=1, keepdims=True)
        energy = jnp.where(column == f, jnp.sqrt(norms / nblock), energy)
        coef = z * lax.rsqrt(norms + EPS)
        lhs = jnp.concatenate(
            [jnp.where(low_half, coef, -coef), pltpu.roll(coef, nblock, 1)], axis=0
        ).astype(jnp.bfloat16)
        m = jnp.dot(lhs, y_ref[f], preferred_element_type=jnp.float32)
        for c in range(ctile):
            out[pl.ds(f * span + c, 2 * nmode, stride=ctile), :] = (
                m[:, c * LANES:(c + 1) * LANES]
            )
        if f > 0:
            store(f - 1).start()
    energy_ref[...] = energy
    store(nbins - 1).start()
    for f in range(nbins):
        store(f).wait()


def shards(n_x, n_y, snapshots, quad_weight, mode_guess, bins, starts):
    length, nvar, cols_x, cols_y = snapshots.shape
    nbins = bins.shape[0]
    nblock = starts.shape[0]
    nmode = mode_guess.shape[-1]
    ctile = nvar * cols_x
    points = ctile * cols_y
    nq = 2 * nbins
    n = n_x * n_y
    grid_points = cols_x * cols_y * n
    vmem = pl.BlockSpec(memory_space=pltpu.VMEM)
    hbm = pl.BlockSpec(memory_space=pltpu.HBM)
    limit = 30 * 1024 * 1024

    x = snapshots.reshape(length * ctile, cols_y)
    guess = jnp.transpose(mode_guess, (0, 2, 3, 1))

    operands = [
        pltpu.with_memory_space_constraint(value, pltpu.HBM)
        for value in (starts, bins, x, quad_weight, guess)
    ]
    per = max(1, nbins * nmode // n)
    dims = (length, nvar, ctile, nblock, nbins, nmode, n_x, n_y, per, grid_points)
    y, z = pl.pallas_call(
        functools.partial(main_kernel, dims),
        name="spod",
        out_shape=(
            jax.ShapeDtypeStruct((nbins, 2 * nblock, points), jnp.bfloat16),
            jax.ShapeDtypeStruct((nbins * nmode, LANES), jnp.float32),
        ),
        in_specs=[hbm] * 5,
        out_specs=(vmem, vmem),
        scratch_shapes=[
            pltpu.SMEM(starts.shape, jnp.int32),
            pltpu.SMEM(bins.shape, jnp.int32),
            pltpu.VMEM(x.shape, jnp.bfloat16),
            pltpu.VMEM(quad_weight.shape, jnp.float32),
            pltpu.VMEM(guess.shape, jnp.float32),
            pltpu.VMEM((nblock * nq, length), jnp.bfloat16),
            pltpu.VMEM((nq, NFFT), jnp.float32),
            pltpu.VMEM((length * ctile, cols_y), jnp.float32),
            pltpu.VMEM((length, points), jnp.bfloat16),
            pltpu.VMEM((1, LANES), jnp.float32),
            pltpu.VMEM((ctile, nblock * nq, LANES), jnp.float32),
            pltpu.VMEM((nbins, 4 * nmode, 2 * nblock), jnp.bfloat16),
            pltpu.VMEM((nbins, 2 * nmode, LANES), jnp.float32),
            pltpu.VMEM((n, 1, LANES), jnp.float32),
            pltpu.VMEM((n, per, LANES), jnp.float32),
            pltpu.VMEM((n, per, LANES), jnp.float32),
            pltpu.VMEM((n, per, LANES), jnp.float32),
            pltpu.SemaphoreType.DMA((5,)),
            pltpu.SemaphoreType.DMA((6,)),
        ],
        compiler_params=pltpu.CompilerParams(
            collective_id=0, has_side_effects=True, vmem_limit_bytes=limit
        ),
    )(*operands)

    modes, energy = pl.pallas_call(
        functools.partial(modes_kernel, (ctile, nblock, nbins, nmode)),
        name="modes",
        out_shape=(
            jax.ShapeDtypeStruct((nbins * 2 * nmode * ctile, cols_y), jnp.float32),
            jax.ShapeDtypeStruct((nmode, nbins), jnp.float32),
        ),
        in_specs=[vmem, vmem],
        out_specs=(hbm, vmem),
        scratch_shapes=[
            pltpu.VMEM((nbins * 2 * nmode * ctile, cols_y), jnp.float32),
            pltpu.SemaphoreType.DMA((nbins,)),
        ],
        compiler_params=pltpu.CompilerParams(vmem_limit_bytes=limit),
    )(y, z)
    return (
        modes.reshape(nbins, 2, nmode, nvar, cols_x, cols_y),
        energy.T,
    )


def solution(mesh):
    n_x, n_y = mesh.shape["sx"], mesh.shape["sy"]
    return jax.shard_map(
        functools.partial(shards, n_x, n_y),
        mesh=mesh,
        in_specs=(P(None, None, "sx", "sy"), P(None, "sx", "sy"), P(), P(), P()),
        out_specs=(P(None, None, None, None, "sx", "sy"), P()),
        check_vma=False,
    )
```

profile of v0, /device:TPU:0, one launch (start us, length us, event | category | flops | bytes accessed | tf_op | source)
XLA Modules:
  0.0 32.3 jit_solution(5188539628773465266)
XLA Ops:
  0.6 29.2 %spod.1 = (bf16[16,128,768]{2,1,0:T(8,128)(2,1)S(1)}, f32[128,128]{1,0:T(8,128)S(1)}) custom-call(s32[64]{0:T(128)} %starts_hbm.1, s32[16]{0:T(128)} %bins_hbm.1, bf16[6144,128]{1,0:T(8,128)(2,1)} %bitcast.4, f32[3,2,128]{2,1,0:T(2,128)} %quad_hbm.1, f32[16,2,8,64]{3,2,1,0:T(8,128)} %bitcast.5), custom_call_target="tpu_custom_call" | custom-call | tf_op jit(solution)/shard_map/spod/pallas_call | solution.py:302
  29.9 2.4 %modes.1 = (f32[1536,128]{1,0:T(8,128)}, f32[8,16]{1,0:T(8,128)}) custom-call(bf16[16,128,768]{2,1,0:T(8,128)(2,1)S(1)} %get-tuple-element.6.y_ref, f32[128,128]{1,0:T(8,128)S(1)} %get-tuple-element.7.z_ref), custom_call_target="tpu_custom_call" | custom-call | tf_op jit(solution)/shard_map/modes/pallas_call | solution.py:337
where the time goes:
time: 32.4 us; the launch traced here: 32.3 us
  Pallas kernels  31.6 us (98%)
  between operations  0.64 us (2%)
    pallas_call x1, Pallas kernels, shards(): pl.pallas_call(functools.partial(main_kernel, dims), name='spod', out_sha...  29.2 us
    pallas_call x1, Pallas kernels, shards(): pl.pallas_call(functools.partial(modes_kernel, (ctile, nblock, nbins, nmo...  2.39 us

commit v1 on v0

v1 whole, which is shorter than its diff:
```python
import functools
import math
import jax
import jax.numpy as jnp
from jax import lax
from jax.experimental import pallas as pl
from jax.experimental.pallas import tpu as pltpu
from jax.sharding import PartitionSpec as P

NFFT = 256
LANES = 128
EPS = 1e-06
MESH = pl.DeviceIdType.MESH


def horner(value, terms):
    total = terms[-1]
    for term in terms[-2::-1]:
        total = total * value + term
    return total


def turn(count):
    wrapped = jnp.where(count < NFFT // 2, count, count - NFFT)
    half = wrapped.astype(jnp.float32) * (math.pi / NFFT)
    sq = half * half
    sin = half * horner(sq, [(-1.0) ** k / math.factorial(2 * k + 1) for k in range(7)])
    cos = horner(sq, [(-1.0) ** k / math.factorial(2 * k) for k in range(8)])
    return 1.0 - 2.0 * sin * sin, 2.0 * sin * cos


def split(value):
    high = value.astype(jnp.bfloat16).astype(jnp.float32)
    return high, value - high


def fill_tables(bins, starts, nbins, nblock, nmode, cos_t, sin_t, cos_b, sin_b, wcat):
    lane = lax.broadcasted_iota(jnp.int32, (8, LANES), 1)
    sub = lax.broadcasted_iota(jnp.int32, (8, LANES), 0)
    row = jnp.zeros((8, LANES), jnp.int32)
    for b in range(nblock):
        row = jnp.where(lane == b, starts[b], row)
    for f in range(nbins):
        at = slice(f * nmode, (f + 1) * nmode)
        cos_b[at, :], sin_b[at, :] = turn(lax.rem(row * bins[f], NFFT))
    shape = (nbins, NFFT)
    which = lax.broadcasted_iota(jnp.int32, shape, 0)
    step = lax.broadcasted_iota(jnp.int32, shape, 1)
    number = jnp.zeros(shape, jnp.int32)
    for f in range(nbins):
        number = jnp.where(which == f, bins[f], number)
    cos, sin = turn(lax.rem(number * step, NFFT))
    for f in range(nbins):
        at = slice(f * nmode, (f + 1) * nmode)
        cos_t[at, :] = jnp.broadcast_to(cos[f:f + 1], (nmode, NFFT))
        sin_t[at, :] = jnp.broadcast_to(sin[f:f + 1], (nmode, NFFT))

    gain = 0.5 * math.sqrt(8.0 / (3.0 * NFFT))
    wave = [turn(lane + j * LANES) for j in range(NFFT // LANES)]
    length = wcat.shape[1]
    for g in range(nblock // 16):
        cols = []
        for h in range(2):
            col = jnp.zeros((8, LANES), jnp.int32)
            for i in range(8):
                col = jnp.where(sub == i, starts[g * 16 + h * 8 + i], col)
            cos_s, sin_s = turn(lax.rem(col, NFFT))
            cols.append((col, cos_s * gain, sin_s * gain))
        for j in range(length // LANES):
            ct, st = wave[j % (NFFT // LANES)]
            parts = []
            for col, cos_s, sin_s in cols:
                since = lane + j * LANES - col
                value = gain - (ct * cos_s + st * sin_s)
                parts.append(jnp.where((since >= 0) & (since < NFFT), value, 0.0))
            high, low = split(jnp.concatenate(parts, axis=0))
            high, low = high.astype(jnp.bfloat16), low.astype(jnp.bfloat16)
            at = slice(j * LANES, (j + 1) * LANES)
            for base, piece in ((0, high), (1, high), (2, low), (3, low)):
                wcat[base * nblock + g * 16:base * nblock + g * 16 + 16, at] = piece


def spread_over_time(nbins, nmode, lhs, wcat, cos_t, sin_t, a_ref):
    both = jnp.concatenate([lhs[...], lhs[...]], axis=1)
    for j in range(wcat.shape[1] // NFFT):
        at = slice(j * NFFT, (j + 1) * NFFT)
        b = jnp.dot(both, wcat[:, at], preferred_element_type=jnp.float32)
        for f in range(nbins):
            rows = slice(f * nmode, (f + 1) * nmode)
            c, s = cos_t[rows, :], sin_t[rows, :]
            re = b[2 * f * nmode:(2 * f + 1) * nmode]
            im = b[(2 * f + 1) * nmode:(2 * f + 2) * nmode]
            a_ref[2 * f * nmode:(2 * f + 2) * nmode, at] = jnp.concatenate(
                [c * re + s * im, c * im - s * re], axis=0
            ).astype(jnp.bfloat16)


def main_kernel(dims, starts_hbm, bins_hbm, x_hbm, quad_hbm, guess_hbm,
                z_ref, xr, wcat, cos_t, sin_t, cols_ref,
                starts, bins, x_ref, quad_ref, guess_ref, xs, cos_b, sin_b, lhs, a_ref,
                sq, sqbuf, zsend, zrecv, zall, load_sems, sems):
    (length, nvar, ctile, nblock, nbins, nmode, n_x, n_y, per, grid_points) = dims
    n = n_x * n_y
    me = lax.axis_index("sx") * n_y + lax.axis_index("sy")
    per_var = ctile // nvar
    loads = [
        pltpu.make_async_copy(src, dst, load_sems.at[i])
        for i, (src, dst) in enumerate(
            [
                (bins_hbm, bins),
                (starts_hbm, starts),
                (guess_hbm, guess_ref),
                (quad_hbm, quad_ref),
                (x_hbm, x_ref),
            ]
        )
    ]
    for load in loads:
        load.start()

    ix, iy = lax.axis_index("sx"), lax.axis_index("sy")

    def each_partner(act):
        def pick(dx, dy):
            tx, ty = lax.rem(ix + dx, n_x), lax.rem(iy + dy, n_y)
            act(tx * n_y + ty, (tx, ty))

        for dy in range(1, n_y):
            pick(0, dy)

        def go(dx, carry):
            for dy in range(n_y):
                pick(dx, dy)
            return carry

        lax.fori_loop(1, n_x, go, 0, unroll=5)

    barrier = pltpu.get_barrier_semaphore()
    each_partner(
        lambda t, where: pl.semaphore_signal(
            barrier, inc=1, device_id=where, device_id_type=MESH
        )
    )

    def spread(src, dst, phase, by_target):
        each_partner(
            lambda t, where: pltpu.make_async_remote_copy(
                src_ref=src.at[t] if by_target else src,
                dst_ref=dst.at[me],
                send_sem=sems.at[2 * phase],
                recv_sem=sems.at[2 * phase + 1],
                device_id=where,
                device_id_type=MESH,
            ).start()
        )

    def wait_all(dst, sem):
        rest = dst.at[pl.ds(0, n - 1)]
        pltpu.make_async_copy(rest, rest, sems.at[sem]).wait()

    with jax.named_scope("tables"):
        loads[0].wait()
        loads[1].wait()
        fill_tables(bins, starts, nbins, nblock, nmode, cos_t, sin_t, cos_b, sin_b, wcat)
    with jax.named_scope("guess"):
        loads[2].wait()
        for f in range(nbins):
            rows = slice(f * nmode, (f + 1) * nmode)
            c, s = cos_b[rows, :nblock], sin_b[rows, :nblock]
            g_re, g_im = guess_ref[f, 0], guess_ref[f, 1]
            value = jnp.concatenate([g_re * c - g_im * s, g_re * s + g_im * c], axis=0)
            high, low = split(value)
            lhs[2 * f * nmode:(2 * f + 2) * nmode, :] = jnp.concatenate(
                [high, low], axis=1
            ).astype(jnp.bfloat16)
    with jax.named_scope("acoef"):
        spread_over_time(nbins, nmode, lhs, wcat, cos_t, sin_t, a_ref)
    with jax.named_scope("loadwait"):
        loads[3].wait()
        loads[4].wait()
    rows = x_ref.shape[0]
    step = rows // 16

    with jax.named_scope("conv"):
        @pl.loop(0, 16)
        def _(i):
            at = pl.ds(pl.multiple_of(i * step, step), step)
            xs[at, :] = x_ref[at, :].astype(jnp.float32)

    lane = lax.broadcasted_iota(jnp.int32, (1, LANES), 1)
    with jax.named_scope("squares"):
        quads = [quad_ref[c // per_var, c % per_var:c % per_var + 1, :] for c in range(ctile)]
        total = jnp.zeros((1, LANES), jnp.float32)
        for c in range(ctile):
            col = xs[pl.ds(c, length, stride=ctile), :]
            xr[:, c * LANES:(c + 1) * LANES] = col.astype(jnp.bfloat16)
            sums = jnp.sum(col * col, axis=0, keepdims=True) * quads[c]
            one = jnp.sum(sums, axis=1, keepdims=True)
            total = total + jnp.where(lane == c // per_var, one, 0.0)
        sq[...] = total

    low_half = lax.broadcasted_iota(jnp.int32, (nmode, LANES), 1) < nblock
    parts = nmode // per
    span = per_var * LANES
    for v in range(nvar):
        with jax.named_scope(f"var{v}"):
            at = slice(v * span, (v + 1) * span)
            weight = jnp.concatenate(quads[v * per_var:(v + 1) * per_var], axis=1)
            u = jnp.dot(a_ref[...], xr[:, at], preferred_element_type=jnp.float32)
            u = (u * weight).astype(jnp.bfloat16)
            acc = None
            for j in range(length // NFFT):
                steps = slice(j * NFFT, (j + 1) * NFFT)
                back = lax.dot_general(
                    u, xr[steps, at], (((1,), (1,)), ((), ())),
                    preferred_element_type=jnp.float32,
                )
                turned = []
                for f in range(nbins):
                    rows = slice(f * nmode, (f + 1) * nmode)
                    c, s = cos_t[rows, :], sin_t[rows, :]
                    re = back[2 * f * nmode:(2 * f + 1) * nmode]
                    im = back[(2 * f + 1) * nmode:(2 * f + 2) * nmode]
                    turned.append(
                        jnp.concatenate([c * re - s * im, s * re + c * im], axis=0).astype(
                            jnp.bfloat16
                        )
                    )
                one = lax.dot_general(
                    jnp.concatenate(turned, axis=0), wcat[nblock:3 * nblock, steps],
                    (((1,), (1,)), ((), ())), preferred_element_type=jnp.float32,
                )
                acc = one if acc is None else acc + one
            acc = (acc + pltpu.roll(acc, nblock, 1)) * (1.0 / (3.0 * grid_points))
            for f in range(nbins):
                z = jnp.where(
                    low_half,
                    acc[2 * f * nmode:(2 * f + 1) * nmode],
                    acc[(2 * f + 1) * nmode:(2 * f + 2) * nmode],
                )
                for s in range(parts):
                    zsend[f * parts + s, v] = z[s * per:(s + 1) * per]
    owners = nbins * parts
    for s in range(owners, n):
        zsend[s] = jnp.zeros((nvar, per, LANES), jnp.float32)

    with jax.named_scope("barrier"):
        pl.semaphore_wait(barrier, n - 1)
    with jax.named_scope("send"):
        spread(sq, sqbuf, 0, False)
        spread(zsend, zrecv, 1, True)
    with jax.named_scope("sqwait"):
        wait_all(sqbuf, 1)
        sqbuf[me] = sq[...]
        total = jnp.sum(sqbuf[...], axis=0)
        scale = lax.rsqrt(total / (length * grid_points) + EPS)
        scales = [
            jnp.sum(jnp.where(lane == v, scale, 0.0), axis=1, keepdims=True) for v in range(nvar)
        ]
        for c in range(ctile):
            cols_ref[c:c + 1, :] = scales[c // per_var] * jnp.sqrt(quads[c])
    with jax.named_scope("a2a"):
        wait_all(zrecv, 3)
    with jax.named_scope("zsum"):
        zrecv[me] = zsend[me]
        sums = jnp.sum(zrecv[...], axis=0)
        z = sums[0] * (scales[0] * scales[0])
        for v in range(1, nvar):
            z = z + sums[v] * (scales[v] * scales[v])
        zall[me] = z
    with jax.named_scope("ag"):
        spread(zall.at[me], zall, 2, False)
        wait_all(zall, 5)
    for s in range(owners):
        z_ref[s * per:(s + 1) * per] = zall[s]
    wait_all(zrecv, 2)
    wait_all(zall, 4)
    wait_all(sqbuf, 0)


def modes_kernel(dims, z_ref, xr, wcat, cos_t, sin_t, cols_ref, modes_hbm, energy_ref,
                 lhs, a_ref, out, sems):
    nvar, ctile, nblock, nbins, nmode = dims
    low_half = lax.broadcasted_iota(jnp.int32, (nmode, LANES), 1) < nblock
    column = lax.broadcasted_iota(jnp.int32, (nmode, nbins), 1)
    energy = jnp.zeros((nmode, nbins), jnp.float32)
    for f in range(nbins):
        z = z_ref[f * nmode:(f + 1) * nmode]
        norms = jnp.sum(z * z, axis=1, keepdims=True)
        energy = jnp.where(column == f, jnp.sqrt(norms / nblock), energy)
        high, low = split(z * lax.rsqrt(norms + EPS))
        lhs[2 * f * nmode:(2 * f + 2) * nmode, :] = jnp.concatenate(
            [
                jnp.where(low_half, high, pltpu.roll(low, nblock, 1)),
                jnp.where(low_half, pltpu.roll(high, nblock, 1), low),
            ],
            axis=0,
        ).astype(jnp.bfloat16)
    energy_ref[...] = energy
    with jax.named_scope("macoef"):
        spread_over_time(nbins, nmode, lhs, wcat, cos_t, sin_t, a_ref)
    per_var = ctile // nvar
    span = per_var * LANES
    rows = 2 * nbins * nmode
    with jax.named_scope("mdot"):
        for v in range(nvar):
            m = jnp.dot(
                a_ref[...], xr[:, v * span:(v + 1) * span], preferred_element_type=jnp.float32
            )
            for k in range(per_var):
                c = v * per_var + k
                out[pl.ds(c, rows, stride=ctile), :] = (
                    m[:, k * LANES:(k + 1) * LANES] * cols_ref[c:c + 1, :]
                )
    with jax.named_scope("mout"):
        copy = pltpu.make_async_copy(out, modes_hbm, sems.at[0])
        copy.start()
        copy.wait()


def shards(n_x, n_y, snapshots, quad_weight, mode_guess, bins, starts):
    length, nvar, cols_x, cols_y = snapshots.shape
    nbins = bins.shape[0]
    nblock = starts.shape[0]
    nmode = mode_guess.shape[-1]
    ctile = nvar * cols_x
    points = ctile * cols_y
    n = n_x * n_y
    grid_points = cols_x * cols_y * n
    vmem = pl.BlockSpec(memory_space=pltpu.VMEM)
    hbm = pl.BlockSpec(memory_space=pltpu.HBM)
    limit = 30 * 1024 * 1024
    rows = 2 * nbins * nmode

    x = snapshots.reshape(length * ctile, cols_y)
    guess = jnp.transpose(mode_guess, (0, 2, 3, 1))

    operands = [
        pltpu.with_memory_space_constraint(value, pltpu.HBM)
        for value in (starts, bins, x, quad_weight, guess)
    ]
    per = max(1, nbins * nmode // n)
    dims = (length, nvar, ctile, nblock, nbins, nmode, n_x, n_y, per, grid_points)
    z, *kept = pl.pallas_call(
        functools.partial(main_kernel, dims),
        name="spod",
        out_shape=(
            jax.ShapeDtypeStruct((nbins * nmode, LANES), jnp.float32),
            jax.ShapeDtypeStruct((length, points), jnp.bfloat16),
            jax.ShapeDtypeStruct((4 * nblock, length), jnp.bfloat16),
            jax.ShapeDtypeStruct((nbins * nmode, NFFT), jnp.float32),
            jax.ShapeDtypeStruct((nbins * nmode, NFFT), jnp.float32),
            jax.ShapeDtypeStruct((8, LANES), jnp.float32),
        ),
        in_specs=[hbm] * 5,
        out_specs=(vmem,) * 6,
        scratch_shapes=[
            pltpu.SMEM(starts.shape, jnp.int32),
            pltpu.SMEM(bins.shape, jnp.int32),
            pltpu.VMEM(x.shape, jnp.bfloat16),
            pltpu.VMEM(quad_weight.shape, jnp.float32),
            pltpu.VMEM(guess.shape, jnp.float32),
            pltpu.VMEM((length * ctile, cols_y), jnp.float32),
            pltpu.VMEM((nbins * nmode, LANES), jnp.float32),
            pltpu.VMEM((nbins * nmode, LANES), jnp.float32),
            pltpu.VMEM((rows, 2 * nblock), jnp.bfloat16),
            pltpu.VMEM((rows, length), jnp.bfloat16),
            pltpu.VMEM((1, LANES), jnp.float32),
            pltpu.VMEM((n, 1, LANES), jnp.float32),
            pltpu.VMEM((n, nvar, per, LANES), jnp.float32),
            pltpu.VMEM((n, nvar, per, LANES), jnp.float32),
            pltpu.VMEM((n, per, LANES), jnp.float32),
            pltpu.SemaphoreType.DMA((5,)),
            pltpu.SemaphoreType.DMA((6,)),
        ],
        compiler_params=pltpu.CompilerParams(
            collective_id=0, has_side_effects=True, vmem_limit_bytes=limit
        ),
    )(*operands)

    modes, energy = pl.pallas_call(
        functools.partial(modes_kernel, (nvar, ctile, nblock, nbins, nmode)),
        name="modes",
        out_shape=(
            jax.ShapeDtypeStruct((rows * ctile, cols_y), jnp.float32),
            jax.ShapeDtypeStruct((nmode, nbins), jnp.float32),
        ),
        in_specs=[vmem] * 6,
        out_specs=(hbm, vmem),
        scratch_shapes=[
            pltpu.VMEM((rows, 2 * nblock), jnp.bfloat16),
            pltpu.VMEM((rows, length), jnp.bfloat16),
            pltpu.VMEM((rows * ctile, cols_y), jnp.float32),
            pltpu.SemaphoreType.DMA((1,)),
        ],
        compiler_params=pltpu.CompilerParams(vmem_limit_bytes=limit),
    )(z, *kept)
    return (
        modes.reshape(nbins, 2, nmode, nvar, cols_x, cols_y),
        energy.T,
    )


def solution(mesh):
    n_x, n_y = mesh.shape["sx"], mesh.shape["sy"]
    return jax.shard_map(
        functools.partial(shards, n_x, n_y),
        mesh=mesh,
        in_specs=(P(None, None, "sx", "sy"), P(None, "sx", "sy"), P(), P(), P()),
        out_specs=(P(None, None, None, None, "sx", "sy"), P()),
        check_vma=False,
    )
```

time: 32.4 us -> 22.3 us (0.69)
  Pallas kernels: 31.6 us -> 21.5 us
    pallas_call x1, Pallas kernels: 29.2 us -> 19 us  [shards(): pl.pallas_call(functools.partial(main_kernel, dims), name='spod', out_sha...]
where the time goes in v1:
time: 22.3 us; the launch traced here: 22.1 us
  Pallas kernels  21.5 us (96%)
  between operations  0.64 us (3%)
    pallas_call x1, Pallas kernels, shards(): pl.pallas_call(functools.partial(main_kernel, dims), name='spod', out_sha...  19 us
    pallas_call x1, Pallas kernels, shards(): pl.pallas_call(functools.partial(modes_kernel, (nvar, ctile, nblock, nbin...  2.5 us

profile of v1, /device:TPU:0, one launch (start us, length us, event | category | flops | bytes accessed | tf_op | source)
XLA Modules:
  0.0 22.1 jit_solution(1529754961154969455)
XLA Ops:
  0.6 19.0 %spod.1 = (f32[128,128]{1,0:T(8,128)S(1)}, bf16[1024,768]{1,0:T(8,128)(2,1)S(1)}, bf16[256,1024]{1,0:T(8,128)(2,1)S(1)}, f32[128,256]{1,0:T(8,128)S(1)}, f32[128,256]{1,0:T(8,128)S(1)}, /*index=5*/f32[8,128]{1,0:T(8,128)S(1)}) custom-call(s32[64]{0:T(128)} %starts_hbm.1, s32[16]{0:T(128)} %bins_hbm.1, bf16[6144,128]{1,0:T(8,128)(2,1)} %bitcast.4, ...), custom_call_target="tpu_custom_call" | custom-call | tf_op jit(solution)/shard_map/spod/pallas_call | solution.py:344
  19.6 2.5 %modes.1 = (f32[1536,128]{1,0:T(8,128)}, f32[8,16]{1,0:T(8,128)}) custom-call(f32[128,128]{1,0:T(8,128)S(1)} %get-tuple-element.10.z_ref, bf16[1024,768]{1,0:T(8,128)(2,1)S(1)} %get-tuple-element.11.xr, bf16[256,1024]{1,0:T(8,128)(2,1)S(1)} %get-tuple-element.12.wcat, f32[128,256]{1,0:T(8,128)S(1)} %get-tuple-element.13.cos_t, ...), custom_call_target="tpu_custom_call" | custom-call | tf_op jit(solution)/shard_map/modes/pallas_call | solution.py:381

commit v2 on v1

--- a/solution.py
+++ b/solution.py
@@ -80,28 +80,37 @@
                 wcat[base * nblock + g * 16:base * nblock + g * 16 + 16, at] = piece
 
 
-def spread_over_time(nbins, nmode, lhs, wcat, cos_t, sin_t, a_ref):
-    both = jnp.concatenate([lhs[...], lhs[...]], axis=1)
-    for j in range(wcat.shape[1] // NFFT):
+def rotate_windows(nbins, nmode, lhs, rhs, cos_t, sin_t, store):
+    for j in range(rhs.shape[1] // NFFT):
         at = slice(j * NFFT, (j + 1) * NFFT)
-        b = jnp.dot(both, wcat[:, at], preferred_element_type=jnp.float32)
+        b = jnp.dot(lhs, rhs[:, at], preferred_element_type=jnp.float32)
         for f in range(nbins):
             rows = slice(f * nmode, (f + 1) * nmode)
             c, s = cos_t[rows, :], sin_t[rows, :]
             re = b[2 * f * nmode:(2 * f + 1) * nmode]
             im = b[(2 * f + 1) * nmode:(2 * f + 2) * nmode]
-            a_ref[2 * f * nmode:(2 * f + 2) * nmode, at] = jnp.concatenate(
-                [c * re + s * im, c * im - s * re], axis=0
-            ).astype(jnp.bfloat16)
+            store(
+                slice(2 * f * nmode, (2 * f + 2) * nmode),
+                j,
+                jnp.concatenate([c * re + s * im, c * im - s * re], axis=0),
+            )
+
+
+def three(value):
+    high, rest = split(value)
+    mid, low = split(rest)
+    return high, mid, low
 
 
 def main_kernel(dims, starts_hbm, bins_hbm, x_hbm, quad_hbm, guess_hbm,
-                z_ref, xr, wcat, cos_t, sin_t, cols_ref,
+                gall, xr, wcat, cos_t, sin_t, roots_ref,
                 starts, bins, x_ref, quad_ref, guess_ref, xs, cos_b, sin_b, lhs, a_ref,
-                sq, sqbuf, zsend, zrecv, zall, load_sems, sems):
-    (length, nvar, ctile, nblock, nbins, nmode, n_x, n_y, per, grid_points) = dims
+                zsend, zrecv, load_sems, sems):
+    (length, nvar, ctile, nblock, nbins, nmode, n_x, n_y, first, grid_points) = dims
     n = n_x * n_y
     me = lax.axis_index("sx") * n_y + lax.axis_index("sy")
+    slot = me - first
+    owner = jnp.logical_and(slot >= 0, slot < nbins)
     per_var = ctile // nvar
     loads = [
         pltpu.make_async_copy(src, dst, load_sems.at[i])
@@ -118,45 +127,34 @@
     for load in loads:
         load.start()
 
-    ix, iy = lax.axis_index("sx"), lax.axis_index("sy")
-
-    def each_partner(act):
-        def pick(dx, dy):
-            tx, ty = lax.rem(ix + dx, n_x), lax.rem(iy + dy, n_y)
-            act(tx * n_y + ty, (tx, ty))
-
-        for dy in range(1, n_y):
-            pick(0, dy)
-
-        def go(dx, carry):
-            for dy in range(n_y):
-                pick(dx, dy)
-            return carry
-
-        lax.fori_loop(1, n_x, go, 0, unroll=5)
+    def each_owner(act):
+        @pl.loop(0, nbins, unroll=4)
+        def _(k):
+            to = lax.rem(me + k, nbins)
+            where = first + to
+
+            @pl.when(where != me)
+            def _():
+                act(to, (where // n_y, lax.rem(where, n_y)))
+
+    def each_other(act):
+        @pl.loop(1, n, unroll=4)
+        def _(k):
+            where = lax.rem(me + k, n)
+            act((where // n_y, lax.rem(where, n_y)))
 
     barrier = pltpu.get_barrier_semaphore()
-    each_partner(
-        lambda t, where: pl.semaphore_signal(
-            barrier, inc=1, device_id=where, device_id_type=MESH
-        )
-    )
-
-    def spread(src, dst, phase, by_target):
-        each_partner(
-            lambda t, where: pltpu.make_async_remote_copy(
-                src_ref=src.at[t] if by_target else src,
-                dst_ref=dst.at[me],
-                send_sem=sems.at[2 * phase],
-                recv_sem=sems.at[2 * phase + 1],
-                device_id=where,
-                device_id_type=MESH,
-            ).start()
-        )
-
-    def wait_all(dst, sem):
-        rest = dst.at[pl.ds(0, n - 1)]
-        pltpu.make_async_copy(rest, rest, sems.at[sem]).wait()
+
+    def greet(where):
+        pl.semaphore_signal(barrier, inc=1, device_id=where, device_id_type=MESH)
+
+    @pl.when(owner)
+    def _():
+        each_other(greet)
+
+    @pl.when(jnp.logical_not(owner))
+    def _():
+        each_owner(lambda to, where: greet(where))
 
     with jax.named_scope("tables"):
         loads[0].wait()
@@ -174,7 +172,12 @@
                 [high, low], axis=1
             ).astype(jnp.bfloat16)
     with jax.named_scope("acoef"):
-        spread_over_time(nbins, nmode, lhs, wcat, cos_t, sin_t, a_ref)
+        def keep(rows, j, value):
+            a_ref[rows, j * NFFT:(j + 1) * NFFT] = value.astype(jnp.bfloat16)
+
+        rotate_windows(
+            nbins, nmode, jnp.concatenate([lhs[...], lhs[...]], axis=1), wcat, cos_t, sin_t, keep
+        )
     with jax.named_scope("loadwait"):
         loads[3].wait()
         loads[4].wait()
@@ -192,16 +195,17 @@
         quads = [quad_ref[c // per_var, c % per_var:c % per_var + 1, :] for c in range(ctile)]
         total = jnp.zeros((1, LANES), jnp.float32)
         for c in range(ctile):
+            roots_ref[c:c + 1, :] = jnp.sqrt(quads[c])
             col = xs[pl.ds(c, length, stride=ctile), :]
             xr[:, c * LANES:(c + 1) * LANES] = col.astype(jnp.bfloat16)
             sums = jnp.sum(col * col, axis=0, keepdims=True) * quads[c]
             one = jnp.sum(sums, axis=1, keepdims=True)
             total = total + jnp.where(lane == c // per_var, one, 0.0)
-        sq[...] = total
 
     low_half = lax.broadcasted_iota(jnp.int32, (nmode, LANES), 1) < nblock
-    parts = nmode // per
+    sub = lax.broadcasted_iota(jnp.int32, (nmode, LANES), 0)
     span = per_var * LANES
+    folded = []
     for v in range(nvar):
         with jax.named_scope(f"var{v}"):
             at = slice(v * span, (v + 1) * span)
@@ -231,86 +235,140 @@
                     (((1,), (1,)), ((), ())), preferred_element_type=jnp.float32,
                 )
                 acc = one if acc is None else acc + one
-            acc = (acc + pltpu.roll(acc, nblock, 1)) * (1.0 / (3.0 * grid_points))
-            for f in range(nbins):
-                z = jnp.where(
-                    low_half,
-                    acc[2 * f * nmode:(2 * f + 1) * nmode],
-                    acc[(2 * f + 1) * nmode:(2 * f + 2) * nmode],
+            folded.append((acc + pltpu.roll(acc, nblock, 1)) * (1.0 / (3.0 * grid_points)))
+    with jax.named_scope("pack"):
+        pieces = jnp.zeros((nmode, LANES), jnp.float32)
+        for i, piece in enumerate(three(total)):
+            pieces = jnp.where(sub == i, piece, pieces)
+        for f in range(nbins):
+            re = slice(2 * f * nmode, (2 * f + 1) * nmode)
+            im = slice((2 * f + 1) * nmode, (2 * f + 2) * nmode)
+            zsend[f] = jnp.concatenate(
+                [jnp.where(low_half, one[re], one[im]) for one in folded] + [pieces], axis=0
+            ).astype(jnp.bfloat16)
+
+    with jax.named_scope("barrier"):
+        pl.semaphore_wait(barrier, jnp.where(owner, n - 1, nbins))
+    with jax.named_scope("send"):
+        each_owner(
+            lambda to, where: pltpu.make_async_remote_copy(
+                src_ref=zsend.at[to],
+                dst_ref=zrecv.at[me],
+                send_sem=sems.at[0],
+                recv_sem=sems.at[1],
+                device_id=where,
+                device_id_type=MESH,
+            ).start()
+        )
+
+    def wait_for(ref, sem):
+        pltpu.make_async_copy(ref, ref, sems.at[sem]).wait()
+
+    @pl.when(owner)
+    def _():
+        with jax.named_scope("a2a"):
+            wait_for(zrecv.at[pl.ds(0, n - 1)], 1)
+        with jax.named_scope("zsum"):
+            zrecv[me] = zsend[slot]
+            sums = jnp.sum(zrecv[...].astype(jnp.float32), axis=0)
+            total = jnp.sum(sums[nvar * nmode:], axis=0, keepdims=True)
+            scale = lax.rsqrt(total / (length * grid_points) + EPS)
+            square = scale * scale
+            z = jnp.zeros((nmode, LANES), jnp.float32)
+            for v in range(nvar):
+                factor = jnp.sum(jnp.where(lane == v, square, 0.0), axis=1, keepdims=True)
+                z = z + sums[v * nmode:(v + 1) * nmode] * factor
+            norms = jnp.sum(z * z, axis=1, keepdims=True)
+            energy = jnp.sqrt(norms / nblock)
+            wide = lax.broadcasted_iota(jnp.int32, (nmode, LANES), 1)
+            extra = jnp.zeros((nmode, LANES), jnp.float32)
+            for i, piece in enumerate(three(energy)):
+                extra = jnp.where(wide == i, piece, extra)
+            for i, piece in enumerate(three(scale)):
+                moved = pltpu.roll(
+                    jnp.broadcast_to(piece, (nmode, LANES)), 3 + i * nvar, 1
                 )
-                for s in range(parts):
-                    zsend[f * parts + s, v] = z[s * per:(s + 1) * per]
-    owners = nbins * parts
-    for s in range(owners, n):
-        zsend[s] = jnp.zeros((nvar, per, LANES), jnp.float32)
-
-    with jax.named_scope("barrier"):
-        pl.semaphore_wait(barrier, n - 1)
-    with jax.named_scope("send"):
-        spread(sq, sqbuf, 0, False)
-        spread(zsend, zrecv, 1, True)
-    with jax.named_scope("sqwait"):
-        wait_all(sqbuf, 1)
-        sqbuf[me] = sq[...]
-        total = jnp.sum(sqbuf[...], axis=0)
-        scale = lax.rsqrt(total / (length * grid_points) + EPS)
-        scales = [
-            jnp.sum(jnp.where(lane == v, scale, 0.0), axis=1, keepdims=True) for v in range(nvar)
-        ]
-        for c in range(ctile):
-            cols_ref[c:c + 1, :] = scales[c // per_var] * jnp.sqrt(quads[c])
-    with jax.named_scope("a2a"):
-        wait_all(zrecv, 3)
-    with jax.named_scope("zsum"):
-        zrecv[me] = zsend[me]
-        sums = jnp.sum(zrecv[...], axis=0)
-        z = sums[0] * (scales[0] * scales[0])
-        for v in range(1, nvar):
-            z = z + sums[v] * (scales[v] * scales[v])
-        zall[me] = z
-    with jax.named_scope("ag"):
-        spread(zall.at[me], zall, 2, False)
-        wait_all(zall, 5)
-    for s in range(owners):
-        z_ref[s * per:(s + 1) * per] = zall[s]
-    wait_all(zrecv, 2)
-    wait_all(zall, 4)
-    wait_all(sqbuf, 0)
-
-
-def modes_kernel(dims, z_ref, xr, wcat, cos_t, sin_t, cols_ref, modes_hbm, energy_ref,
-                 lhs, a_ref, out, sems):
-    nvar, ctile, nblock, nbins, nmode = dims
+                inside = jnp.logical_and(wide >= 3 + i * nvar, wide < 3 + (i + 1) * nvar)
+                extra = jnp.where(inside, moved, extra)
+            gall[slot] = jnp.concatenate([z * lax.rsqrt(norms + EPS), extra], axis=0).astype(
+                jnp.bfloat16
+            )
+        with jax.named_scope("agsend"):
+            each_other(
+                lambda where: pltpu.make_async_remote_copy(
+                    src_ref=gall.at[slot],
+                    dst_ref=gall.at[slot],
+                    send_sem=sems.at[2],
+                    recv_sem=sems.at[3],
+                    device_id=where,
+                    device_id_type=MESH,
+                ).start()
+            )
+        with jax.named_scope("ag"):
+            wait_for(gall.at[pl.ds(0, nbins - 1)], 3)
+            wait_for(zsend.at[pl.ds(0, nbins - 1)], 0)
+            for _ in range((n - 1) // (nbins - 1)):
+                wait_for(gall.at[pl.ds(0, nbins - 1)], 2)
+            rest = (n - 1) % (nbins - 1)
+            if rest:
+                wait_for(gall.at[pl.ds(0, rest)], 2)
+
+    @pl.when(jnp.logical_not(owner))
+    def _():
+        with jax.named_scope("ag"):
+            wait_for(gall, 3)
+            wait_for(zsend, 0)
+
+
+def modes_kernel(dims, gall, xr, wcat, cos_t, sin_t, roots_ref, modes_hbm, energy_ref,
+                 a_ref, out, sems):
+    length, nvar, ctile, nblock, nbins, nmode = dims
     low_half = lax.broadcasted_iota(jnp.int32, (nmode, LANES), 1) < nblock
+    lane = lax.broadcasted_iota(jnp.int32, (nmode, LANES), 1)
     column = lax.broadcasted_iota(jnp.int32, (nmode, nbins), 1)
     energy = jnp.zeros((nmode, nbins), jnp.float32)
+    lhs = []
     for f in range(nbins):
-        z = z_ref[f * nmode:(f + 1) * nmode]
-        norms = jnp.sum(z * z, axis=1, keepdims=True)
-        energy = jnp.where(column == f, jnp.sqrt(norms / nblock), energy)
-        high, low = split(z * lax.rsqrt(norms + EPS))
-        lhs[2 * f * nmode:(2 * f + 2) * nmode, :] = jnp.concatenate(
-            [
-                jnp.where(low_half, high, pltpu.roll(low, nblock, 1)),
-                jnp.where(low_half, pltpu.roll(high, nblock, 1), low),
-            ],
-            axis=0,
-        ).astype(jnp.bfloat16)
+        message = gall[f].astype(jnp.float32)
+        coef, extra = message[:nmode], message[nmode:]
+        one = jnp.sum(jnp.where(lane < 3, extra, 0.0), axis=1, keepdims=True)
+        energy = jnp.where(column == f, one, energy)
+        swapped = pltpu.roll(coef, nblock, 1)
+        lhs.append(
+            jnp.concatenate(
+                [jnp.where(low_half, coef, swapped), jnp.where(low_half, swapped, coef)], axis=0
+            ).astype(jnp.bfloat16)
+        )
     energy_ref[...] = energy
+    extra = gall[0].astype(jnp.float32)[nmode:nmode + 1]
+    scales = []
+    for v in range(nvar):
+        mine = jnp.zeros((1, LANES), jnp.bool_)
+        for i in range(3):
+            mine = jnp.logical_or(mine, lane[:1] == 3 + i * nvar + v)
+        scales.append(jnp.sum(jnp.where(mine, extra, 0.0), axis=1, keepdims=True))
     with jax.named_scope("macoef"):
-        spread_over_time(nbins, nmode, lhs, wcat, cos_t, sin_t, a_ref)
+        def keep(rows, j, value):
+            high, low = split(value)
+            a_ref[rows, j * NFFT:(j + 1) * NFFT] = high.astype(jnp.bfloat16)
+            a_ref[rows, length + j * NFFT:length + (j + 1) * NFFT] = low.astype(jnp.bfloat16)
+
+        rotate_windows(
+            nbins, nmode, jnp.concatenate(lhs, axis=0), wcat.at[nblock:3 * nblock],
+            cos_t, sin_t, keep
+        )
     per_var = ctile // nvar
     span = per_var * LANES
     rows = 2 * nbins * nmode
     with jax.named_scope("mdot"):
         for v in range(nvar):
-            m = jnp.dot(
-                a_ref[...], xr[:, v * span:(v + 1) * span], preferred_element_type=jnp.float32
-            )
+            at = slice(v * span, (v + 1) * span)
+            m = jnp.dot(a_ref[:, :length], xr[:, at], preferred_element_type=jnp.float32)
+            m = m + jnp.dot(a_ref[:, length:], xr[:, at], preferred_element_type=jnp.float32)
             for k in range(per_var):
                 c = v * per_var + k
-                out[pl.ds(c, rows, stride=ctile), :] = (
-                    m[:, k * LANES:(k + 1) * LANES] * cols_ref[c:c + 1, :]
+                out[pl.ds(c, rows, stride=ctile), :] = m[:, k * LANES:(k + 1) * LANES] * (
+                    scales[v] * roots_ref[c:c + 1, :]
                 )
     with jax.named_scope("mout"):
         copy = pltpu.make_async_copy(out, modes_hbm, sems.at[0])
@@ -339,13 +397,13 @@
         pltpu.with_memory_space_constraint(value, pltpu.HBM)
         for value in (starts, bins, x, quad_weight, guess)
     ]
-    per = max(1, nbins * nmode // n)
-    dims = (length, nvar, ctile, nblock, nbins, nmode, n_x, n_y, per, grid_points)
-    z, *kept = pl.pallas_call(
+    first = (n - nbins) // 2
+    dims = (length, nvar, ctile, nblock, nbins, nmode, n_x, n_y, first, grid_points)
+    gall, *kept = pl.pallas_call(
         functools.partial(main_kernel, dims),
         name="spod",
         out_shape=(
-            jax.ShapeDtypeStruct((nbins * nmode, LANES), jnp.float32),
+            jax.ShapeDtypeStruct((nbins, 2 * nmode, LANES), jnp.bfloat16),
             jax.ShapeDtypeStruct((length, points), jnp.bfloat16),
             jax.ShapeDtypeStruct((4 * nblock, length), jnp.bfloat16),
             jax.ShapeDtypeStruct((nbins * nmode, NFFT), jnp.float32),
@@ -365,13 +423,10 @@
             pltpu.VMEM((nbins * nmode, LANES), jnp.float32),
             pltpu.VMEM((rows, 2 * nblock), jnp.bfloat16),
             pltpu.VMEM((rows, length), jnp.bfloat16),
-            pltpu.VMEM((1, LANES), jnp.float32),
-            pltpu.VMEM((n, 1, LANES), jnp.float32),
-            pltpu.VMEM((n, nvar, per, LANES), jnp.float32),
-            pltpu.VMEM((n, nvar, per, LANES), jnp.float32),
-            pltpu.VMEM((n, per, LANES), jnp.float32),
+            pltpu.VMEM((nbins, (nvar + 1) * nmode, LANES), jnp.bfloat16),
+            pltpu.VMEM((n, (nvar + 1) * nmode, LANES), jnp.bfloat16),
             pltpu.SemaphoreType.DMA((5,)),
-            pltpu.SemaphoreType.DMA((6,)),
+            pltpu.SemaphoreType.DMA((4,)),
         ],
         compiler_params=pltpu.CompilerParams(
             collective_id=0, has_side_effects=True, vmem_limit_bytes=limit
@@ -379,7 +434,7 @@
     )(*operands)
 
     modes, energy = pl.pallas_call(
-        functools.partial(modes_kernel, (nvar, ctile, nblock, nbins, nmode)),
+        functools.partial(modes_kernel, (length, nvar, ctile, nblock, nbins, nmode)),
         name="modes",
         out_shape=(
             jax.ShapeDtypeStruct((rows * ctile, cols_y), jnp.float32),
@@ -388,13 +443,12 @@
         in_specs=[vmem] * 6,
         out_specs=(hbm, vmem),
         scratch_shapes=[
-            pltpu.VMEM((rows, 2 * nblock), jnp.bfloat16),
-            pltpu.VMEM((rows, length), jnp.bfloat16),
+            pltpu.VMEM((rows, 2 * length), jnp.bfloat16),
             pltpu.VMEM((rows * ctile, cols_y), jnp.float32),
             pltpu.SemaphoreType.DMA((1,)),
         ],
         compiler_params=pltpu.CompilerParams(vmem_limit_bytes=limit),
-    )(z, *kept)
+    )(gall, *kept)
     return (
         modes.reshape(nbins, 2, nmode, nvar, cols_x, cols_y),
         energy.T,

time: 22.3 us -> 20.8 us (0.933)
  Pallas kernels: 21.5 us -> 19.9 us
    pallas_call x1, Pallas kernels: 19 us -> 17.1 us  [shards(): pl.pallas_call(functools.partial(main_kernel, dims), name='spod', out_sha...]
    pallas_call x1, Pallas kernels: 2.5 us -> 2.84 us  [shards(): pl.pallas_call(functools.partial(modes_kernel, (length, nvar, ctile, nblo...]
where the time goes in v2:
time: 20.8 us; the launch traced here: 20.6 us
  Pallas kernels  19.9 us (96%)
  between operations  0.64 us (3%)
    pallas_call x1, Pallas kernels, shards(): pl.pallas_call(functools.partial(main_kernel, dims), name='spod', out_sha...  17.1 us
    pallas_call x1, Pallas kernels, shards(): pl.pallas_call(functools.partial(modes_kernel, (length, nvar, ctile, nblo...  2.84 us

profile of v2, /device:TPU:0, one launch (start us, length us, event | category | flops | bytes accessed | tf_op | source)
XLA Modules:
  0.0 20.6 jit_solution(17143447249882613935)
XLA Ops:
  0.6 17.1 %spod.1 = (bf16[16,16,128]{2,1,0:T(8,128)(2,1)S(1)}, bf16[1024,768]{1,0:T(8,128)(2,1)S(1)}, bf16[256,1024]{1,0:T(8,128)(2,1)S(1)}, f32[128,256]{1,0:T(8,128)S(1)...) custom-call(s32[64]{0:T(128)} %starts_hbm.1, s32[16]{0:T(128)} %bins_hbm.1, bf16[6144,128]{1,0:T(8,128)(2,1)} %bitcast.4, ...), custom_call_target="tpu_custom_call" | custom-call | tf_op jit(solution)/shard_map/spod/pallas_call | solution.py:402
  17.7 2.8 %modes.1 = (f32[1536,128]{1,0:T(8,128)}, f32[8,16]{1,0:T(8,128)}) custom-call(bf16[16,16,128]{2,1,0:T(8,128)(2,1)S(1)} %get-tuple-element.10.gall, bf16[1024,768]{1,0:T(8,128)(2,1)S(1)} %get-tuple-element.11.xr, bf16[256,1024]{1,0:T(8,128)(2,1)S(1)} %get-tuple-element.12.wcat, f32[128,256]{1,0:T(8,128)S(1)} %get-tuple-element.13.cos_t, ...), custom_call_target="tpu_custom_call" | custom-call | tf_op jit(solution)/shard_map/modes/pallas_call | solution.py:436

commit v3 on v2

--- a/solution.py
+++ b/solution.py
@@ -96,16 +96,10 @@
             )
 
 
-def three(value):
-    high, rest = split(value)
-    mid, low = split(rest)
-    return high, mid, low
-
-
 def main_kernel(dims, starts_hbm, bins_hbm, x_hbm, quad_hbm, guess_hbm,
-                gall, xr, wcat, cos_t, sin_t, roots_ref,
-                starts, bins, x_ref, quad_ref, guess_ref, xs, cos_b, sin_b, lhs, a_ref,
-                zsend, zrecv, load_sems, sems):
+                modes_ref, energy_ref,
+                starts, bins, x_ref, quad_ref, guess_ref, xs, xr, wcat, cos_t, sin_t, cos_b, sin_b,
+                lhs, a_ref, zsend, zrecv, sqsend, sqrecv, zall, scale_ref, load_sems, sems):
     (length, nvar, ctile, nblock, nbins, nmode, n_x, n_y, first, grid_points) = dims
     n = n_x * n_y
     me = lax.axis_index("sx") * n_y + lax.axis_index("sy")
@@ -127,21 +121,28 @@
     for load in loads:
         load.start()
 
+    base = jnp.where(owner, slot, lax.rem(me, nbins))
+    nonowner = jnp.logical_not(owner)
+
     def each_owner(act):
-        @pl.loop(0, nbins, unroll=4)
-        def _(k):
-            to = lax.rem(me + k, nbins)
+        def pick(k):
+            to = lax.rem(base + k, nbins)
             where = first + to
-
+            act(to, (where // n_y, lax.rem(where, n_y)))
+
+        for k in range(1, nbins):
+            pick(k)
+
+        @pl.when(nonowner)
+        def _():
+            pick(0)
+
+    def each_other(act):
+        @pl.loop(0, n, unroll=8)
+        def _(where):
             @pl.when(where != me)
             def _():
-                act(to, (where // n_y, lax.rem(where, n_y)))
-
-    def each_other(act):
-        @pl.loop(1, n, unroll=4)
-        def _(k):
-            where = lax.rem(me + k, n)
-            act((where // n_y, lax.rem(where, n_y)))
+                act((where // n_y, lax.rem(where, n_y)))
 
     barrier = pltpu.get_barrier_semaphore()
 
@@ -152,7 +153,7 @@
     def _():
         each_other(greet)
 
-    @pl.when(jnp.logical_not(owner))
+    @pl.when(nonowner)
     def _():
         each_owner(lambda to, where: greet(where))
 
@@ -195,17 +196,28 @@
         quads = [quad_ref[c // per_var, c % per_var:c % per_var + 1, :] for c in range(ctile)]
         total = jnp.zeros((1, LANES), jnp.float32)
         for c in range(ctile):
-            roots_ref[c:c + 1, :] = jnp.sqrt(quads[c])
             col = xs[pl.ds(c, length, stride=ctile), :]
             xr[:, c * LANES:(c + 1) * LANES] = col.astype(jnp.bfloat16)
             sums = jnp.sum(col * col, axis=0, keepdims=True) * quads[c]
             one = jnp.sum(sums, axis=1, keepdims=True)
             total = total + jnp.where(lane == c // per_var, one, 0.0)
 
+        sqsend[...] = total
+
+    def send(src, dst, number):
+        each_owner(
+            lambda to, where: pltpu.make_async_remote_copy(
+                src_ref=src(to),
+                dst_ref=dst,
+                send_sem=sems.at[2 * number],
+                recv_sem=sems.at[2 * number + 1],
+                device_id=where,
+                device_id_type=MESH,
+            ).start()
+        )
+
     low_half = lax.broadcasted_iota(jnp.int32, (nmode, LANES), 1) < nblock
-    sub = lax.broadcasted_iota(jnp.int32, (nmode, LANES), 0)
     span = per_var * LANES
-    folded = []
     for v in range(nvar):
         with jax.named_scope(f"var{v}"):
             at = slice(v * span, (v + 1) * span)
@@ -235,144 +247,173 @@
                     (((1,), (1,)), ((), ())), preferred_element_type=jnp.float32,
                 )
                 acc = one if acc is None else acc + one
-            folded.append((acc + pltpu.roll(acc, nblock, 1)) * (1.0 / (3.0 * grid_points)))
-    with jax.named_scope("pack"):
-        pieces = jnp.zeros((nmode, LANES), jnp.float32)
-        for i, piece in enumerate(three(total)):
-            pieces = jnp.where(sub == i, piece, pieces)
-        for f in range(nbins):
-            re = slice(2 * f * nmode, (2 * f + 1) * nmode)
-            im = slice((2 * f + 1) * nmode, (2 * f + 2) * nmode)
-            zsend[f] = jnp.concatenate(
-                [jnp.where(low_half, one[re], one[im]) for one in folded] + [pieces], axis=0
-            ).astype(jnp.bfloat16)
-
-    with jax.named_scope("barrier"):
-        pl.semaphore_wait(barrier, jnp.where(owner, n - 1, nbins))
-    with jax.named_scope("send"):
-        each_owner(
-            lambda to, where: pltpu.make_async_remote_copy(
-                src_ref=zsend.at[to],
-                dst_ref=zrecv.at[me],
-                send_sem=sems.at[0],
-                recv_sem=sems.at[1],
-                device_id=where,
-                device_id_type=MESH,
-            ).start()
-        )
-
+            acc = (acc + pltpu.roll(acc, nblock, 1)) * (1.0 / (3.0 * grid_points))
+            for f in range(nbins):
+                re = slice(2 * f * nmode, (2 * f + 1) * nmode)
+                im = slice((2 * f + 1) * nmode, (2 * f + 2) * nmode)
+                zsend[v, f] = jnp.where(low_half, acc[re], acc[im]).astype(jnp.bfloat16)
+        if v == 0:
+            with jax.named_scope("barrier"):
+                pl.semaphore_wait(barrier, jnp.where(owner, n - 1, nbins))
+            send(lambda to: sqsend, sqrecv.at[me], nvar)
+        with jax.named_scope("send"):
+            send(lambda to, v=v: zsend.at[v, to], zrecv.at[v, me], v)
+
+    gathered = 2 * nvar + 2
     def wait_for(ref, sem):
         pltpu.make_async_copy(ref, ref, sems.at[sem]).wait()
+
+    half = nbins // 2
 
     @pl.when(owner)
     def _():
         with jax.named_scope("a2a"):
-            wait_for(zrecv.at[pl.ds(0, n - 1)], 1)
-        with jax.named_scope("zsum"):
-            zrecv[me] = zsend[slot]
-            sums = jnp.sum(zrecv[...].astype(jnp.float32), axis=0)
-            total = jnp.sum(sums[nvar * nmode:], axis=0, keepdims=True)
+            wait_for(sqrecv.at[pl.ds(0, n - 1)], 2 * nvar + 1)
+            sqrecv[me] = sqsend[...]
+            total = jnp.sum(sqrecv[...], axis=0)
             scale = lax.rsqrt(total / (length * grid_points) + EPS)
+            scale_ref[...] = scale
             square = scale * scale
             z = jnp.zeros((nmode, LANES), jnp.float32)
             for v in range(nvar):
+                wait_for(zrecv.at[v, pl.ds(0, n - 1)], 2 * v + 1)
+                zrecv[v, me] = zsend[v, slot]
                 factor = jnp.sum(jnp.where(lane == v, square, 0.0), axis=1, keepdims=True)
-                z = z + sums[v * nmode:(v + 1) * nmode] * factor
-            norms = jnp.sum(z * z, axis=1, keepdims=True)
-            energy = jnp.sqrt(norms / nblock)
-            wide = lax.broadcasted_iota(jnp.int32, (nmode, LANES), 1)
-            extra = jnp.zeros((nmode, LANES), jnp.float32)
-            for i, piece in enumerate(three(energy)):
-                extra = jnp.where(wide == i, piece, extra)
-            for i, piece in enumerate(three(scale)):
-                moved = pltpu.roll(
-                    jnp.broadcast_to(piece, (nmode, LANES)), 3 + i * nvar, 1
-                )
-                inside = jnp.logical_and(wide >= 3 + i * nvar, wide < 3 + (i + 1) * nvar)
-                extra = jnp.where(inside, moved, extra)
-            gall[slot] = jnp.concatenate([z * lax.rsqrt(norms + EPS), extra], axis=0).astype(
-                jnp.bfloat16
-            )
+                z = z + jnp.sum(zrecv[v].astype(jnp.float32), axis=0) * factor
+        with jax.named_scope("zsum"):
+            zall[slot] = z.astype(jnp.bfloat16)
         with jax.named_scope("agsend"):
             each_other(
                 lambda where: pltpu.make_async_remote_copy(
-                    src_ref=gall.at[slot],
-                    dst_ref=gall.at[slot],
-                    send_sem=sems.at[2],
-                    recv_sem=sems.at[3],
+                    src_ref=zall.at[slot],
+                    dst_ref=zall.at[slot],
+                    send_sem=sems.at[gathered],
+                    recv_sem=sems.at[gathered + 1 + slot // half],
                     device_id=where,
                     device_id_type=MESH,
                 ).start()
             )
-        with jax.named_scope("ag"):
-            wait_for(gall.at[pl.ds(0, nbins - 1)], 3)
-            wait_for(zsend.at[pl.ds(0, nbins - 1)], 0)
-            for _ in range((n - 1) // (nbins - 1)):
-                wait_for(gall.at[pl.ds(0, nbins - 1)], 2)
-            rest = (n - 1) % (nbins - 1)
+            for k in range((n - nbins) // nbins):
+                rank = slot + k * nbins
+                where = jnp.where(rank < first, rank, rank + nbins)
+                pltpu.make_async_remote_copy(
+                    src_ref=scale_ref,
+                    dst_ref=scale_ref,
+                    send_sem=sems.at[gathered + 3],
+                    recv_sem=sems.at[gathered + 4],
+                    device_id=(where // n_y, lax.rem(where, n_y)),
+                    device_id_type=MESH,
+                ).start()
+
+    roots = [jnp.sqrt(quads[c]) for c in range(ctile)]
+    count = half * nmode
+    column = lax.broadcasted_iota(jnp.int32, (nmode, nbins), 1)
+
+    def finish(group):
+        mine = jnp.logical_and(owner, slot // half == group)
+
+        with jax.named_scope("agwait"):
+            @pl.when(mine)
+            def _():
+                wait_for(zall.at[pl.ds(0, half - 1)], gathered + 1 + group)
+
+            @pl.when(jnp.logical_not(mine))
+            def _():
+                wait_for(zall.at[pl.ds(0, half)], gathered + 1 + group)
+
+        with jax.named_scope("macoef"):
+            rows_l = []
+            energy = energy_ref[...]
+            for i in range(half):
+                f = group * half + i
+                z = zall[f].astype(jnp.float32)
+                norms = jnp.sum(z * z, axis=1, keepdims=True)
+                energy = jnp.where(column == f, jnp.sqrt(norms / nblock), energy)
+                coef = z * lax.rsqrt(norms + EPS)
+                swapped = pltpu.roll(coef, nblock, 1)
+                rows_l.append(
+                    jnp.concatenate(
+                        [jnp.where(low_half, coef, swapped), jnp.where(low_half, swapped, coef)],
+                        axis=0,
+                    ).astype(jnp.bfloat16)
+                )
+            energy_ref[...] = energy
+
+            def keep(rows, j, value):
+                high, low = split(value)
+                at = slice(j * NFFT, (j + 1) * NFFT)
+                a_ref[rows, at] = high.astype(jnp.bfloat16)
+                a_ref[slice(2 * count + rows.start, 2 * count + rows.stop), at] = low.astype(
+                    jnp.bfloat16
+                )
+
+            table = pl.ds(pl.multiple_of(group * count, count), count)
+            rotate_windows(
+                half, nmode, jnp.concatenate(rows_l, axis=0), wcat.at[nblock:3 * nblock],
+                cos_t.at[table], sin_t.at[table], keep
+            )
+        return mine
+
+    def multiply(group, scales):
+        with jax.named_scope("mdot"):
+            for v in range(nvar):
+                at = slice(v * span, (v + 1) * span)
+                m = jnp.dot(a_ref[...], xr[:, at], preferred_element_type=jnp.float32)
+                m = m[:2 * count] + m[2 * count:]
+                for k in range(per_var):
+                    c = v * per_var + k
+                    modes_ref[pl.ds(group * (2 * count * ctile) + c, 2 * count, stride=ctile), :] = (
+                        m[:, k * LANES:(k + 1) * LANES] * (scales[v] * roots[c])
+                    )
+
+    energy_ref[...] = jnp.zeros((nmode, nbins), jnp.float32)
+    near = jnp.where(me < n // 2, 0, 1)
+    with jax.named_scope("scalewait"):
+        @pl.when(nonowner)
+        def _():
+            wait_for(scale_ref, gathered + 4)
+    scale = scale_ref[...]
+    scales = [jnp.sum(jnp.where(lane == v, scale, 0.0), axis=1, keepdims=True) for v in range(nvar)]
+
+    @pl.loop(0, 2)
+    def _(i):
+        group = jnp.where(i == 0, near, 1 - near)
+        finish(group)
+        multiply(group, scales)
+
+    with jax.named_scope("drain"):
+        @pl.when(owner)
+        def _():
+            for v in range(nvar):
+                wait_for(zsend.at[v, pl.ds(0, nbins - 1)], 2 * v)
+            wait_for(sqrecv.at[pl.ds(0, nbins - 1)], 2 * nvar)
+            for _ in range((n - 1) // nbins):
+                wait_for(zall, gathered)
+            rest = (n - 1) % nbins
             if rest:
-                wait_for(gall.at[pl.ds(0, rest)], 2)
-
-    @pl.when(jnp.logical_not(owner))
-    def _():
-        with jax.named_scope("ag"):
-            wait_for(gall, 3)
-            wait_for(zsend, 0)
-
-
-def modes_kernel(dims, gall, xr, wcat, cos_t, sin_t, roots_ref, modes_hbm, energy_ref,
-                 a_ref, out, sems):
-    length, nvar, ctile, nblock, nbins, nmode = dims
-    low_half = lax.broadcasted_iota(jnp.int32, (nmode, LANES), 1) < nblock
-    lane = lax.broadcasted_iota(jnp.int32, (nmode, LANES), 1)
-    column = lax.broadcasted_iota(jnp.int32, (nmode, nbins), 1)
-    energy = jnp.zeros((nmode, nbins), jnp.float32)
-    lhs = []
-    for f in range(nbins):
-        message = gall[f].astype(jnp.float32)
-        coef, extra = message[:nmode], message[nmode:]
-        one = jnp.sum(jnp.where(lane < 3, extra, 0.0), axis=1, keepdims=True)
-        energy = jnp.where(column == f, one, energy)
-        swapped = pltpu.roll(coef, nblock, 1)
-        lhs.append(
-            jnp.concatenate(
-                [jnp.where(low_half, coef, swapped), jnp.where(low_half, swapped, coef)], axis=0
-            ).astype(jnp.bfloat16)
+                wait_for(zall.at[pl.ds(0, rest)], gathered)
+            for _ in range((n - nbins) // nbins):
+                wait_for(scale_ref, gathered + 3)
+
+        @pl.when(nonowner)
+        def _():
+            for v in range(nvar):
+                wait_for(zsend.at[v], 2 * v)
+            wait_for(sqrecv.at[pl.ds(0, nbins)], 2 * nvar)
+
+
+def copy_kernel(pieces, value, energy, out_hbm, energy_hbm, sems):
+    size = value.shape[0] // pieces
+    copies = [
+        pltpu.make_async_copy(
+            value.at[pl.ds(i * size, size)], out_hbm.at[pl.ds(i * size, size)], sems.at[i]
         )
-    energy_ref[...] = energy
-    extra = gall[0].astype(jnp.float32)[nmode:nmode + 1]
-    scales = []
-    for v in range(nvar):
-        mine = jnp.zeros((1, LANES), jnp.bool_)
-        for i in range(3):
-            mine = jnp.logical_or(mine, lane[:1] == 3 + i * nvar + v)
-        scales.append(jnp.sum(jnp.where(mine, extra, 0.0), axis=1, keepdims=True))
-    with jax.named_scope("macoef"):
-        def keep(rows, j, value):
-            high, low = split(value)
-            a_ref[rows, j * NFFT:(j + 1) * NFFT] = high.astype(jnp.bfloat16)
-            a_ref[rows, length + j * NFFT:length + (j + 1) * NFFT] = low.astype(jnp.bfloat16)
-
-        rotate_windows(
-            nbins, nmode, jnp.concatenate(lhs, axis=0), wcat.at[nblock:3 * nblock],
-            cos_t, sin_t, keep
-        )
-    per_var = ctile // nvar
-    span = per_var * LANES
-    rows = 2 * nbins * nmode
-    with jax.named_scope("mdot"):
-        for v in range(nvar):
-            at = slice(v * span, (v + 1) * span)
-            m = jnp.dot(a_ref[:, :length], xr[:, at], preferred_element_type=jnp.float32)
-            m = m + jnp.dot(a_ref[:, length:], xr[:, at], preferred_element_type=jnp.float32)
-            for k in range(per_var):
-                c = v * per_var + k
-                out[pl.ds(c, rows, stride=ctile), :] = m[:, k * LANES:(k + 1) * LANES] * (
-                    scales[v] * roots_ref[c:c + 1, :]
-                )
-    with jax.named_scope("mout"):
-        copy = pltpu.make_async_copy(out, modes_hbm, sems.at[0])
+        for i in range(pieces)
+    ]
+    copies.append(pltpu.make_async_copy(energy, energy_hbm, sems.at[pieces]))
+    for copy in copies:
         copy.start()
+    for copy in copies:
         copy.wait()
 
 
@@ -399,19 +440,15 @@
     ]
     first = (n - nbins) // 2
     dims = (length, nvar, ctile, nblock, nbins, nmode, n_x, n_y, first, grid_points)
-    gall, *kept = pl.pallas_call(
+    modes, energy = pl.pallas_call(
         functools.partial(main_kernel, dims),
         name="spod",
         out_shape=(
-            jax.ShapeDtypeStruct((nbins, 2 * nmode, LANES), jnp.bfloat16),
-            jax.ShapeDtypeStruct((length, points), jnp.bfloat16),
-            jax.ShapeDtypeStruct((4 * nblock, length), jnp.bfloat16),
-            jax.ShapeDtypeStruct((nbins * nmode, NFFT), jnp.float32),
-            jax.ShapeDtypeStruct((nbins * nmode, NFFT), jnp.float32),
-            jax.ShapeDtypeStruct((8, LANES), jnp.float32),
+            jax.ShapeDtypeStruct((rows * ctile, cols_y), jnp.float32),
+            jax.ShapeDtypeStruct((nmode, nbins), jnp.float32),
         ),
         in_specs=[hbm] * 5,
-        out_specs=(vmem,) * 6,
+        out_specs=(vmem, vmem),
         scratch_shapes=[
             pltpu.SMEM(starts.shape, jnp.int32),
             pltpu.SMEM(bins.shape, jnp.int32),
@@ -419,36 +456,41 @@
             pltpu.VMEM(quad_weight.shape, jnp.float32),
             pltpu.VMEM(guess.shape, jnp.float32),
             pltpu.VMEM((length * ctile, cols_y), jnp.float32),
+            pltpu.VMEM((length, points), jnp.bfloat16),
+            pltpu.VMEM((4 * nblock, length), jnp.bfloat16),
+            pltpu.VMEM((nbins * nmode, NFFT), jnp.float32),
+            pltpu.VMEM((nbins * nmode, NFFT), jnp.float32),
             pltpu.VMEM((nbins * nmode, LANES), jnp.float32),
             pltpu.VMEM((nbins * nmode, LANES), jnp.float32),
             pltpu.VMEM((rows, 2 * nblock), jnp.bfloat16),
             pltpu.VMEM((rows, length), jnp.bfloat16),
-            pltpu.VMEM((nbins, (nvar + 1) * nmode, LANES), jnp.bfloat16),
-            pltpu.VMEM((n, (nvar + 1) * nmode, LANES), jnp.bfloat16),
+            pltpu.VMEM((nvar, nbins, nmode, LANES), jnp.bfloat16),
+            pltpu.VMEM((nvar, n, nmode, LANES), jnp.bfloat16),
+            pltpu.VMEM((1, LANES), jnp.float32),
+            pltpu.VMEM((n, 1, LANES), jnp.float32),
+            pltpu.VMEM((nbins, nmode, LANES), jnp.bfloat16),
+            pltpu.VMEM((1, LANES), jnp.float32),
             pltpu.SemaphoreType.DMA((5,)),
-            pltpu.SemaphoreType.DMA((4,)),
+            pltpu.SemaphoreType.DMA((2 * nvar + 7,)),
         ],
         compiler_params=pltpu.CompilerParams(
             collective_id=0, has_side_effects=True, vmem_limit_bytes=limit
         ),
     )(*operands)
 
+    pieces = 1
     modes, energy = pl.pallas_call(
-        functools.partial(modes_kernel, (length, nvar, ctile, nblock, nbins, nmode)),
-        name="modes",
+        functools.partial(copy_kernel, pieces),
+        name="store",
         out_shape=(
-            jax.ShapeDtypeStruct((rows * ctile, cols_y), jnp.float32),
-            jax.ShapeDtypeStruct((nmode, nbins), jnp.float32),
+            jax.ShapeDtypeStruct(modes.shape, jnp.float32),
+            jax.ShapeDtypeStruct(energy.shape, jnp.float32),
         ),
-        in_specs=[vmem] * 6,
-        out_specs=(hbm, vmem),
-        scratch_shapes=[
-            pltpu.VMEM((rows, 2 * length), jnp.bfloat16),
-            pltpu.VMEM((rows * ctile, cols_y), jnp.float32),
-            pltpu.SemaphoreType.DMA((1,)),
-        ],
+        in_specs=[vmem, vmem],
+        out_specs=(hbm, hbm),
+        scratch_shapes=[pltpu.SemaphoreType.DMA((pieces + 1,))],
         compiler_params=pltpu.CompilerParams(vmem_limit_bytes=limit),
-    )(gall, *kept)
+    )(modes, energy)
     return (
         modes.reshape(nbins, 2, nmode, nvar, cols_x, cols_y),
         energy.T,

time: 20.8 us -> 20.1 us (0.966)
  Pallas kernels: 19.9 us -> 19.3 us
    pallas_call x1, Pallas kernels: 2.84 us -> 0.9 us  [shards(): pl.pallas_call(functools.partial(copy_kernel, pieces), name='store', out_...]
    pallas_call x1, Pallas kernels: 17.1 us -> 18.4 us  [shards(): pl.pallas_call(functools.partial(main_kernel, dims), name='spod', out_sha...]
where the time goes in v3:
time: 20.1 us; the launch traced here: 19.9 us
  Pallas kernels  19.3 us (96%)
  between operations  0.64 us (3%)
    pallas_call x1, Pallas kernels, shards(): pl.pallas_call(functools.partial(main_kernel, dims), name='spod', out_sha...  18.4 us
    pallas_call x1, Pallas kernels, shards(): pl.pallas_call(functools.partial(copy_kernel, pieces), name='store', out_...  0.9 us

profile of v3, /device:TPU:0, one launch (start us, length us, event | category | flops | bytes accessed | tf_op | source)
XLA Modules:
  0.0 19.9 jit_solution(10822089595230788104)
XLA Ops:
  0.6 18.4 %spod.1 = (f32[1536,128]{1,0:T(8,128)S(1)}, f32[8,16]{1,0:T(8,128)S(1)}) custom-call(s32[64]{0:T(128)} %starts_hbm.1, s32[16]{0:T(128)} %bins_hbm.1, bf16[6144,128]{1,0:T(8,128)(2,1)} %bitcast.4, f32[3,2,128]{2,1,0:T(2,128)} %quad_hbm.1, f32[16,2,8,64]{3,2,1,0:T(8,128)} %bitcast.5), custom_call_target="tpu_custom_call" | custom-call | tf_op jit(solution)/shard_map/spod/pallas_call | solution.py:443
  19.0 0.9 %store.1 = (f32[1536,128]{1,0:T(8,128)}, f32[8,16]{1,0:T(8,128)}) custom-call(f32[1536,128]{1,0:T(8,128)S(1)} %get-tuple-element.6.value, f32[8,16]{1,0:T(8,128)S(1)} %get-tuple-element.7.energy), custom_call_target="tpu_custom_call" | custom-call | tf_op jit(solution)/shard_map/store/pallas_call | solution.py:482
